TPU v7x, 512 devices: a whole 4x4x16 slice. The times are simulated.
512 devices in a mesh: dp: 32 (over y, x, core), ctx: 16 (over z).
Axes of the slice: x: 4, y: 4, z: 16, core: 2. Of those that a mesh axis runs over, the one named last changes fastest.
Arguments:
- q_src: bfloat16 [65536, 4096], P(('dp', 'ctx')), may hold values from -40 to 40
- kv_src: bfloat16 [65536, 1024], P(('dp', 'ctx')), may hold values from -40 to 40
- route: int32 [65536, 1], replicated, may hold values from 0 to 31; in each aligned block of 2048 rows (0 to 2047, 2048 to 4095, ...) at most 96 rows name the same one
- doc_ids: int32 [32, 3072], P('dp'), may hold values from 0 to 5, never falling along the last dimension, each value on 1 to 1024 neighbouring positions
Outputs:
- attended: bfloat16 [98304, 4096], P(('dp', 'ctx'))
Inputs may be any that keep to these rules, and one draw needn't show every extreme that they name: `route`: within each source group's 2048 rows (aligned blocks of 2048 rows), no sequence is named by more than 96 rows, a bound that some block reaches. `doc_ids`: never falling along a sequence; every document has 1 to 1024 slots and one has exactly 1024.
All inputs are finite; a program needn't handle non-finite values.
Results may differ from a plain program's by a relative error of at most 0.011.
Values may be sent and summed in bfloat16 or wider, within the bound.
A program may use at most 64 MiB of HBM per device.

v0:
```python
import math

import jax
import jax.numpy as jnp
from jax import lax
from jax.sharding import PartitionSpec as P

Q_HEADS = 32
KV_HEADS = 4
HEAD_DIM = 128


def attend(queries, kv_pairs, doc_rows, live_rows, kv_local):
    pack_len = queries.shape[0]
    head_count = queries.shape[1] // HEAD_DIM
    group_size = head_count // kv_local
    block_len = math.gcd(pack_len, 512)
    doc_most = pack_len // 3
    window = min(pack_len, doc_most + block_len)
    score_scale = HEAD_DIM ** (-0.5)
    grouped = queries.reshape(pack_len, kv_local, group_size, HEAD_DIM)
    split_pairs = kv_pairs.reshape(pack_len, 2, kv_local, HEAD_DIM)

    def one_block(block_index):
        row_start = block_index * block_len
        key_start = jnp.maximum(row_start + block_len - window, 0)
        query_block = lax.dynamic_slice_in_dim(grouped, row_start, block_len, 0)
        key_block = lax.dynamic_slice_in_dim(split_pairs, key_start, window, 0)
        query_docs = lax.dynamic_slice_in_dim(doc_rows, row_start, block_len, 0)
        key_docs = lax.dynamic_slice_in_dim(doc_rows, key_start, window, 0)
        query_pos = row_start + jnp.arange(block_len, dtype=jnp.int32)
        key_pos = key_start + jnp.arange(window, dtype=jnp.int32)
        allowed = (query_docs[:, None] == key_docs[None, :]) & (
            key_pos[None, :] <= query_pos[:, None]
        )
        scores = (
            jnp.einsum(
                "qkgd,skd->kgqs", query_block, key_block[:, 0], preferred_element_type=jnp.float32
            )
            * score_scale
        )
        masked = jnp.where(allowed, scores, -1e30)
        row_max = jnp.max(masked, axis=-1, keepdims=True)
        exponent = jnp.where(allowed, jnp.exp(masked - row_max), 0.0)
        probs = exponent / jnp.sum(exponent, axis=-1, keepdims=True)
        weights = probs.astype(jnp.bfloat16)
        mixed = jnp.einsum(
            "kgqs,skd->qkgd", weights, key_block[:, 1], preferred_element_type=jnp.float32
        )
        mixed = jnp.where((query_pos < live_rows)[:, None, None, None], mixed, 0.0)
        return mixed.astype(jnp.bfloat16).reshape(block_len, head_count * HEAD_DIM)

    blocks = lax.map(one_block, jnp.arange(pack_len // block_len, dtype=jnp.int32))
    return blocks.reshape(pack_len, head_count * HEAD_DIM)


def on_device(q_src, kv_src, route, doc_ids):
    ctx_size = lax.axis_size("ctx")
    dp_size = lax.axis_size("dp")
    rows_dev = q_src.shape[0]
    heads_dev = Q_HEADS // ctx_size
    kv_rows = kv_src.reshape(rows_dev, 2, KV_HEADS, HEAD_DIM)
    wide_pairs = jnp.repeat(kv_rows, Q_HEADS // KV_HEADS, axis=2)
    wide_pairs = wide_pairs.reshape(rows_dev, 2, ctx_size, heads_dev * HEAD_DIM)
    wide_pairs = wide_pairs.transpose(0, 2, 1, 3).reshape(
        rows_dev, ctx_size * 2 * heads_dev * HEAD_DIM
    )
    queries, kv_pairs = (
        lax.all_to_all(q_src, "ctx", split_axis=1, concat_axis=0, tiled=True),
        lax.all_to_all(wide_pairs, "ctx", split_axis=1, concat_axis=0, tiled=True),
    )
    length = rows_dev * ctx_size
    capacity = 3 * length // (2 * dp_size)
    pack_len = dp_size * capacity
    pack_plan = route.reshape(dp_size, length)
    seq_ids = jnp.arange(dp_size, dtype=jnp.int32)
    counts = jnp.sum((pack_plan[:, :, None] == seq_ids[None, None, :]).astype(jnp.int32), axis=1)
    own_index = lax.axis_index("dp")
    own_plan = lax.dynamic_slice_in_dim(pack_plan, own_index, 1, 0)[0]
    onehot = (own_plan[:, None] == seq_ids[None, :]).astype(jnp.int32)
    slot_rank = jnp.sum((jnp.cumsum(onehot, axis=0) - onehot) * onehot, axis=1)
    target = own_plan * capacity + slot_rank
    send_q = jnp.zeros((pack_len, queries.shape[1]), jnp.bfloat16).at[target].set(queries)
    send_kv = jnp.zeros((pack_len, kv_pairs.shape[1]), jnp.bfloat16).at[target].set(kv_pairs)
    recv_q, recv_kv = (
        lax.all_to_all(
            send_q.reshape(dp_size, capacity, -1), "dp", split_axis=0, concat_axis=0, tiled=True
        ),
        lax.all_to_all(
            send_kv.reshape(dp_size, capacity, -1), "dp", split_axis=0, concat_axis=0, tiled=True
        ),
    )
    incoming = lax.dynamic_slice_in_dim(counts, own_index, 1, 1)[:, 0]
    starts = jnp.cumsum(incoming) - incoming
    live_rows = jnp.sum(incoming)
    packed_pos = jnp.arange(pack_len, dtype=jnp.int32)
    source_idx = jnp.sum((starts[None, :] <= packed_pos[:, None]).astype(jnp.int32), axis=1) - 1
    offset = jnp.minimum(packed_pos - jnp.take(starts, source_idx), capacity - 1)
    gather_idx = source_idx * capacity + offset
    packed_q = jnp.take(recv_q.reshape(pack_len, -1), gather_idx, axis=0)
    packed_kv = jnp.take(recv_kv.reshape(pack_len, -1), gather_idx, axis=0)
    attended = attend(packed_q, packed_kv, doc_ids[0], live_rows, heads_dev)
    return lax.all_to_all(attended, "ctx", split_axis=0, concat_axis=1, tiled=True)


def solution(mesh):
    in_specs = (P(("dp", "ctx"), None), P(("dp", "ctx"), None), P(), P("dp", None))
    out_specs = P(("dp", "ctx"), None)
    return jax.shard_map(
        on_device, mesh=mesh, in_specs=in_specs, out_specs=out_specs, check_vma=False
    )
```

profile of v0, /device:TPU:1, one launch (start us, length us, event | category | flops | bytes accessed | tf_op | source)
XLA Modules:
  0.0 439.8 jit_solution(17130107149010776909)
XLA Ops:
  0.0 2.3 copy.50
  2.3 15.7 %all-to-all-start.2 = ((bf16[128,16,256]{0,2,1:T(8,128)(2,1)}), bf16[128,16,256]{0,2,1:T(8,128)(2,1)S(1)}, u32[]{:S(2)}, u32[]{:S(2)}) async-start(bf16[128,16,256]{0,2,1:T(8,128)(2,1)} %bitcast.64), calls=%async_computation.2 | async-start | bytes 2097152 | tf_op jit(solution)/shard_map/all_to_all | solution.py:69
  18.7 1.5 copy.47
  20.3 42.7 %all-to-all-done.2 = bf16[128,16,256]{0,2,1:T(8,128)(2,1)S(1)} async-done(((bf16[128,16,256]{0,2,1:T(8,128)(2,1)}), bf16[128,16,256]{0,2,1:T(8,128)(2,1)S(1)}, u32[]{:S(2)}, u32[]{:S(2)}) %all-to-all-start.2) | async-done | bytes 1048608 | tf_op jit(solution)/shard_map/all_to_all | solution.py:69
  62.9 13.2 %all-to-all-start = ((bf16[128,16,512]{0,2,1:T(8,128)(2,1)}), bf16[128,16,512]{0,2,1:T(8,128)(2,1)S(1)}, u32[]{:S(2)}, u32[]{:S(2)}) async-start(bf16[128,16,512]{0,2,1:T(8,128)(2,1)} %bitcast.162), calls=%async_computation | async-start | bytes 4194304 | tf_op jit(solution)/shard_map/all_to_all | solution.py:70
  76.6 2.0 reduce.69
  78.6 1.0 eq.71
  81.0 15.9 %reduce-window.18 = s32[32,16,128]{2,1,0:T(8,128)S(1)} reduce-window(s32[32,16,128]{2,1,0:T(8,128)} %fusion.28, s32[]{:T(128)} %constant.144.clone.1), window={size=1x1x128 pad=0_0x0_0x127_0}, to_apply=%region_3.4 | reduce-window | flops 8323072 | bytes 524292 | tf_op jit(solution)/shard_map/reduce-window.1
  96.9 0.8 slice.128
  97.8 1.2 copy.57
  99.4 0.9 compare_select_fusion.8
  100.3 1.3 copy.51
  101.6 11.0 %scatter_custom_fusion.1 = bf16[3072,256]{1,0:T(8,128)(2,1)} fusion(s32[2048]{0:T(1024)S(1)} %bitcast.185, bf16[2048,256]{1,0:T(8,128)(2,1)} %bitcast.171, bf16[]{:T(256)} %constant.145.clone.1), kind=kCustom, calls=%fused_computation.35 | custom fusion | bytes 1573376 | tf_op jit(solution)/shard_map/scatter | solution.py:83
  112.6 55.4 %all-to-all-done = bf16[128,16,512]{0,2,1:T(8,128)(2,1)S(1)} async-done(((bf16[128,16,512]{0,2,1:T(8,128)(2,1)}), bf16[128,16,512]{0,2,1:T(8,128)(2,1)S(1)}, u32[]{:S(2)}, u32[]{:S(2)}) %all-to-all-start) | async-done | bytes 2097184 | tf_op jit(solution)/shard_map/all_to_all | solution.py:70
  168.0 1.3 copy-done.2
  169.3 11.4 %all-to-all-start.3 = ((bf16[32,96,256]{2,1,0:T(8,128)(2,1)}), bf16[32,96,256]{2,1,0:T(8,128)(2,1)S(1)}, u32[]{:S(2)}, u32[]{:S(2)}) async-start(bf16[32,96,256]{2,1,0:T(8,128)(2,1)} %bitcast.165), calls=%async_computation.3 | async-start | bytes 3145728 | tf_op jit(solution)/shard_map/all_to_all | solution.py:86
  180.7 1.1 convert_reduce_fusion
  183.4 3.9 copy.48
  187.3 12.1 %scatter_custom_fusion = bf16[3072,512]{1,0:T(8,128)(2,1)} fusion(s32[2048]{0:T(1024)S(1)} %bitcast.186, bf16[2048,512]{1,0:T(8,128)(2,1)} %bitcast.168, bf16[]{:T(256)} %constant.145.clone.1), kind=kCustom, calls=%fused_computation.33 | custom fusion | bytes 3146240 | tf_op jit(solution)/shard_map/scatter | solution.py:84
  199.4 3.5 all-to-all-done.3
  202.9 1.1 copy-done.1
  204.0 5.9 %all-to-all-start.1 = ((bf16[32,96,512]{2,1,0:T(8,128)(2,1)}), bf16[32,96,512]{2,1,0:T(8,128)(2,1)S(1)}, u32[]{:S(2)}, u32[]{:S(2)}) async-start(bf16[32,96,512]{2,1,0:T(8,128)(2,1)} %bitcast.160), calls=%async_computation.1 | async-start | bytes 6291456 | tf_op jit(solution)/shard_map/all_to_all | solution.py:89
  210.7 4.3 compare_select_fusion.2
  215.0 0.9 compare_reduce_fusion.24
  215.9 15.7 %compare_and_fusion.1 = (pred[3072]{0:T(1024)(128)(4,1)S(1)}, s32[3072]{0:T(1024)S(1)}) fusion(s32[3072]{0:T(1024)S(1)} %convert_reduce_fusion.1, pred[3072]{0:T(1024)(128)(4,1)S(1)} %get-tuple-element.171, pred[3072]{0:T(1024)(128)(4,1)S(1)} %get-tuple-element.169, pred[3072]{0:T(1024)(128)(4,1)S(1)} %get-tuple-element.170, ...), kind=kLoop, calls=%fused_computation.86 | loop fusion | flops 132096 | bytes 116836 | tf_op jit(solution)/shard_map/jit(_take)/and | solution.py:100
  231.7 13.7 %gather_fusion.1 = bf16[3072,256]{1,0:T(8,128)(2,1)} fusion(bf16[3072,256]{1,0:T(8,128)(2,1)} %bitcast.159, s32[3072]{0:T(1024)S(1)} %broadcast_clamp_fusion), kind=kCustom, calls=%fused_computation.1 | custom fusion | bytes 3158016 | tf_op jit(solution)/shard_map/jit(_take)/gather | solution.py:100
  245.4 3.5 gather.23
  248.9 3.9 copy_select_fusion.1
  252.9 13.2 %gather_fusion = bf16[3072,512]{1,0:T(8,128)(2,1)} fusion(bf16[3072,512]{1,0:T(8,128)(2,1)S(1)} %bitcast.158, s32[3072]{0:T(1024)S(1)} %broadcast_clamp_fusion), kind=kCustom, calls=%fused_computation | custom fusion | bytes 6303744 | tf_op jit(solution)/shard_map/jit(_take)/gather | solution.py:101
  266.1 3.8 gather.21
  269.8 3.7 copy_select_fusion
  273.5 90.0 %while.14 = (s32[]{:T(128)}, bf16[6,512,256]{2,1,0:T(8,128)(2,1)}, s32[6]{0:T(128)S(1)}, s32[]{:T(128)}, bf16[3072,2,2,128]{3,0,2,1:T(8,128)(2,1)}, /*index=5*/s...) while((s32[]{:T(128)}, bf16[6,512,256]{2,1,0:T(8,128)(2,1)}, ...), condition=%wide.region_12.13_spmd, body=%wide.region_9.12_spmd.sunk | while | flops 829948928 | bytes 50394908 | solution.py:53
  275.0 1.2 compare_and_fusion.3
  276.2 2.7 fusion.39
  278.9 1.7 fusion.40
  280.6 1.0 copy-done
  282.1 5.5 %fusion.41 = bf16[2,128,1,512]{3,1,0,2:T(8,128)(2,1)S(1)} fusion(f32[2,512]{1,0:T(2,128)S(1)} %fusion.40, f32[2,512]{1,0:T(2,128)S(1)} %get-tuple-element.276, f32[2,1536,512]{2,1,0:T(8,128)} %copy-done, pred[512,1536]{0,1:T(8,128)(4,1)S(1)} %compare_and_fusion.3, bf16[3072,2,2,128]{3,0,2,1:T(8,128)(2,1)} %get-tuple-element.307, s32[]{:T(128)S(6)} %max.10, ...), kind=kOutput, calls=%fused_computation.14.clone.1 | convolution fusion | flops 412352512 | bytes 8135176 | tf_op jit(solution)/shard_map/while/body/eval_jaxpr/kgqs,skd->qkgd/dot_general | solution.py:47
  290.0 1.2 compare_and_fusion.3
  291.2 2.7 fusion.39
  293.9 1.7 fusion.40
  295.6 1.0 copy-done
  297.1 5.5 %fusion.41 = bf16[2,128,1,512]{3,1,0,2:T(8,128)(2,1)S(1)} fusion(f32[2,512]{1,0:T(2,128)S(1)} %fusion.40, f32[2,512]{1,0:T(2,128)S(1)} %get-tuple-element.276, f32[2,1536,512]{2,1,0:T(8,128)} %copy-done, pred[512,1536]{0,1:T(8,128)(4,1)S(1)} %compare_and_fusion.3, bf16[3072,2,2,128]{3,0,2,1:T(8,128)(2,1)} %get-tuple-element.307, s32[]{:T(128)S(6)} %max.10, ...), kind=kOutput, calls=%fused_computation.14.clone.1 | convolution fusion | flops 412352512 | bytes 8135176 | tf_op jit(solution)/shard_map/while/body/eval_jaxpr/kgqs,skd->qkgd/dot_general | solution.py:47
  305.0 1.2 compare_and_fusion.3
  306.2 2.7 fusion.39
  308.9 1.7 fusion.40
  310.6 1.0 copy-done
  312.1 5.5 %fusion.41 = bf16[2,128,1,512]{3,1,0,2:T(8,128)(2,1)S(1)} fusion(f32[2,512]{1,0:T(2,128)S(1)} %fusion.40, f32[2,512]{1,0:T(2,128)S(1)} %get-tuple-element.276, f32[2,1536,512]{2,1,0:T(8,128)} %copy-done, pred[512,1536]{0,1:T(8,128)(4,1)S(1)} %compare_and_fusion.3, bf16[3072,2,2,128]{3,0,2,1:T(8,128)(2,1)} %get-tuple-element.307, s32[]{:T(128)S(6)} %max.10, ...), kind=kOutput, calls=%fused_computation.14.clone.1 | convolution fusion | flops 412352512 | bytes 8135176 | tf_op jit(solution)/shard_map/while/body/eval_jaxpr/kgqs,skd->qkgd/dot_general | solution.py:47
  320.0 1.2 compare_and_fusion.3
  321.2 2.7 fusion.39
  323.9 1.7 fusion.40
  325.6 1.0 copy-done
  327.1 5.5 %fusion.41 = bf16[2,128,1,512]{3,1,0,2:T(8,128)(2,1)S(1)} fusion(f32[2,512]{1,0:T(2,128)S(1)} %fusion.40, f32[2,512]{1,0:T(2,128)S(1)} %get-tuple-element.276, f32[2,1536,512]{2,1,0:T(8,128)} %copy-done, pred[512,1536]{0,1:T(8,128)(4,1)S(1)} %compare_and_fusion.3, bf16[3072,2,2,128]{3,0,2,1:T(8,128)(2,1)} %get-tuple-element.307, s32[]{:T(128)S(6)} %max.10, ...), kind=kOutput, calls=%fused_computation.14.clone.1 | convolution fusion | flops 412352512 | bytes 8135176 | tf_op jit(solution)/shard_map/while/body/eval_jaxpr/kgqs,skd->qkgd/dot_general | solution.py:47
  335.0 1.2 compare_and_fusion.3
  336.2 2.7 fusion.39
  338.9 1.7 fusion.40
  340.6 1.0 copy-done
  342.1 5.5 %fusion.41 = bf16[2,128,1,512]{3,1,0,2:T(8,128)(2,1)S(1)} fusion(f32[2,512]{1,0:T(2,128)S(1)} %fusion.40, f32[2,512]{1,0:T(2,128)S(1)} %get-tuple-element.276, f32[2,1536,512]{2,1,0:T(8,128)} %copy-done, pred[512,1536]{0,1:T(8,128)(4,1)S(1)} %compare_and_fusion.3, bf16[3072,2,2,128]{3,0,2,1:T(8,128)(2,1)} %get-tuple-element.307, s32[]{:T(128)S(6)} %max.10, ...), kind=kOutput, calls=%fused_computation.14.clone.1 | convolution fusion | flops 412352512 | bytes 8135176 | tf_op jit(solution)/shard_map/while/body/eval_jaxpr/kgqs,skd->qkgd/dot_general | solution.py:47
  350.0 1.2 compare_and_fusion.3
  351.2 2.7 fusion.39
  353.9 1.7 fusion.40
  355.6 1.0 copy-done
  357.1 5.5 %fusion.41 = bf16[2,128,1,512]{3,1,0,2:T(8,128)(2,1)S(1)} fusion(f32[2,512]{1,0:T(2,128)S(1)} %fusion.40, f32[2,512]{1,0:T(2,128)S(1)} %get-tuple-element.276, f32[2,1536,512]{2,1,0:T(8,128)} %copy-done, pred[512,1536]{0,1:T(8,128)(4,1)S(1)} %compare_and_fusion.3, bf16[3072,2,2,128]{3,0,2,1:T(8,128)(2,1)} %get-tuple-element.307, s32[]{:T(128)S(6)} %max.10, ...), kind=kOutput, calls=%fused_computation.14.clone.1 | convolution fusion | flops 412352512 | bytes 8135176 | tf_op jit(solution)/shard_map/while/body/eval_jaxpr/kgqs,skd->qkgd/dot_general | solution.py:47
  363.5 75.0 %all_to_all.67 = bf16[16,192,256]{2,1,0:T(8,128)(2,1)S(1)} all-to-all(bf16[16,192,256]{2,1,0:T(8,128)(2,1)} %bitcast.169), channel_id=1, replica_groups=mesh['dp'=32,'ctx'=16] {'ctx'}, dimensions={0} | all-to-all | bytes 3145728 | tf_op jit(solution)/shard_map/all_to_all | solution.py:103
  438.5 1.3 copy.61
  (86 shorter events, 18.7 us)
Async XLA Ops:
  0.0 18.1 %copy-start.6 = (bf16[128,1024]{1,0:T(8,128)(2,1)S(1)}, bf16[128,1024]{1,0:T(8,128)(2,1)}, u32[]{:S(2)}) copy-start(bf16[128,1024]{1,0:T(8,128)(2,1)} %param.7) | copy-start | bytes 786436
  2.3 60.6 %all-to-all-start.2 = ((bf16[128,16,256]{0,2,1:T(8,128)(2,1)}), bf16[128,16,256]{0,2,1:T(8,128)(2,1)S(1)}, u32[]{:S(2)}, u32[]{:S(2)}) async-start(bf16[128,16,256]{0,2,1:T(8,128)(2,1)} %bitcast.64), calls=%async_computation.2 | async-start | bytes 2097152 | tf_op jit(solution)/shard_map/all_to_all | solution.py:69
  20.2 56.4 %copy-start.5 = (s32[65536,1]{0,1:T(1,128)S(1)}, s32[65536,1]{0,1:T(1,128)}, u32[]{:S(2)}) copy-start(s32[65536,1]{0,1:T(1,128)} %param.8) | copy-start | bytes 786436
  62.9 105.1 %all-to-all-start = ((bf16[128,16,512]{0,2,1:T(8,128)(2,1)}), bf16[128,16,512]{0,2,1:T(8,128)(2,1)S(1)}, u32[]{:S(2)}, u32[]{:S(2)}) async-start(bf16[128,16,512]{0,2,1:T(8,128)(2,1)} %bitcast.162), calls=%async_computation | async-start | bytes 4194304 | tf_op jit(solution)/shard_map/all_to_all | solution.py:70
  79.6 0.7 copy-start.3
  100.3 80.4 %copy-start.4 = (s32[32,2048]{1,0:T(8,128)S(1)}, s32[32,2048]{1,0:T(8,128)}, u32[]{:S(2)}) copy-start(s32[32,2048]{1,0:T(8,128)} %copy-done.3) | copy-start | bytes 786436
  168.0 1.4 copy-start.2
  169.3 33.6 %all-to-all-start.3 = ((bf16[32,96,256]{2,1,0:T(8,128)(2,1)}), bf16[32,96,256]{2,1,0:T(8,128)(2,1)S(1)}, u32[]{:S(2)}, u32[]{:S(2)}) async-start(bf16[32,96,256]{2,1,0:T(8,128)(2,1)} %bitcast.165), calls=%async_computation.3 | async-start | bytes 3145728 | tf_op jit(solution)/shard_map/all_to_all | solution.py:86
  202.9 1.1 copy-start.1
  204.0 48.8 %all-to-all-start.1 = ((bf16[32,96,512]{2,1,0:T(8,128)(2,1)}), bf16[32,96,512]{2,1,0:T(8,128)(2,1)S(1)}, u32[]{:S(2)}, u32[]{:S(2)}) async-start(bf16[32,96,512]{2,1,0:T(8,128)(2,1)} %bitcast.160), calls=%async_computation.1 | async-start | bytes 6291456 | tf_op jit(solution)/shard_map/all_to_all | solution.py:89
  269.8 3.7 copy-start.7
  278.9 2.7 copy-start
  293.9 2.7 copy-start
  308.9 2.7 copy-start
  323.9 2.7 copy-start
  338.9 2.7 copy-start
  353.9 2.7 copy-start
where the time goes:
time: 448 us; the launch traced here: 440 us
  waiting for transfers between devices  102 us (23%)
  local copies, waits for them, and re-layouts  92 us (21%)
  blocking collectives  75 us (17%)
  other arithmetic  71 us (16%)
  matrix products  49.4 us (11%)
  starting transfers between devices  46.2 us (10%)
    all_to_all x1, blocking collectives, on_device(): lax.all_to_all(attended, 'ctx', split_axis=0, concat_axis=1, tiled=True)  75 us
    all_to_all x1, waiting for transfers between devices, on_device(): lax.all_to_all(wide_pairs, 'ctx', split_axis=1, concat_axis=0, tiled=True)  55.4 us
    all_to_all x1, waiting for transfers between devices, on_device(): lax.all_to_all(q_src, 'ctx', split_axis=1, concat_axis=0, tiled=True)  42.7 us
    dot_general x6, matrix products, one_block(): jnp.einsum('kgqs,skd->qkgd', weights, key_block[:, 1], preferred_element_...  33 us
    gather x2, local copies, waits for them, and re-layouts, on_device(): packed_q = jnp.take(recv_q.reshape(pack_len, -1), gather_idx, axis=0)  17.2 us
    gather x2, local copies, waits for them, and re-layouts, on_device(): packed_kv = jnp.take(recv_kv.reshape(pack_len, -1), gather_idx, axis=0)  17 us
    dot_general x6, matrix products, one_block(): jnp.einsum('qkgd,skd->kgqs', query_block, key_block[:, 0], preferred_elem...  16.4 us
    another operation x4, other arithmetic  16.3 us
  transfers between devices with their start and end apart: 4, of which 3 were waited for; matrix products, arithmetic and copies ran while one was open for 23% of the time, Pallas kernels for 0%

commit v1 on v0

v1 whole, which is shorter than its diff:
```python
import functools

import jax
import jax.numpy as jnp
from jax import lax
from jax.experimental import pallas as pl
from jax.experimental.pallas import tpu as pltpu
from jax.sharding import PartitionSpec as P

Q_HEADS = 32
KV_HEADS = 4
HEAD_DIM = 128
DOC_MOST = 1024
BLOCK = 256
BATCH = 4
NEG = -1e30
MESH = pl.DeviceIdType.MESH
BF16 = jnp.bfloat16
F32 = jnp.float32
I32 = jnp.int32


class Sizes:
    def __init__(self, dp, ctx, rows, cap, heads, kv_heads, doc_most, block):
        self.dp, self.ctx, self.rows, self.cap = dp, ctx, rows, cap
        self.heads, self.kv_heads = heads, kv_heads
        self.local = heads // ctx
        self.team = ctx // kv_heads
        self.group = rows * ctx
        self.pack = dp * cap
        self.slots = self.pack // ctx
        self.part = rows // self.team
        self.lanes = self.group // 128
        self.tiles = self.pack // 128
        self.doc_most, self.block = doc_most, block
        self.blocks = self.pack // block
        self.window = doc_most + block
        self.batches = dp // BATCH


def iota(shape, dim):
    return lax.broadcasted_iota(I32, shape, dim)


def alternating(n):
    order = []
    for k in range(1, n // 2):
        order += [k, n - k]
    return order + [n // 2]


def kernel(
    z, route_ref, doc_ref, q_hbm, kv_hbm, out_ref,
    qg, kvg, send_q, send_kv, recv_q, recv_kv, pq, pkv, ob, pick, place,
    target, pos, key_doc, query_doc, live_col,
    zq_s, zq_r, k1_s, k1_r, k2_s, k2_r, dkv_s, dkv_r, dq_s, dq_r, o_s, o_r, own,
):
    g = lax.axis_index("dp")
    c = lax.axis_index("ctx")
    nz, nd, hd = z.ctx, z.dp, HEAD_DIM
    quarter = lax.rem(c, z.team)
    quad = c - quarter

    barrier = pltpu.get_barrier_semaphore()

    def greet(axis, me, n):
        def body(k, _):
            pl.semaphore_signal(
                barrier, inc=1, device_id={axis: lax.rem(me + k, n)}, device_id_type=MESH
            )
            return 0

        lax.fori_loop(1, n, body, 0)

    greet("ctx", c, nz)
    greet("dp", g, nd)
    pl.semaphore_wait(barrier, nz + nd - 2)

    def remote(src, dst, s, r, axis, peer):
        return pltpu.make_async_remote_copy(
            src_ref=src, dst_ref=dst, send_sem=s, recv_sem=r,
            device_id={axis: peer}, device_id_type=MESH,
        )

    def kv_cut(half, peer):
        part = lax.rem(peer, z.team)
        head = peer // z.team
        rows = pl.ds(pl.multiple_of(part * z.part, z.part), z.part)
        cols = pl.ds(pl.multiple_of((half * z.kv_heads + head) * hd, hd), hd)
        return kv_hbm.at[rows, cols], part

    def kv_one(half, peer):
        src, part = kv_cut(half, peer)
        dst = kvg.at[c, part, :, pl.ds(half * hd, hd)]
        return remote(src, dst, k1_s.at[half, peer], k1_r.at[half, c], "ctx", peer)

    def kv_one_in(half, peer):
        dst = kvg.at[peer, quarter, :, pl.ds(half * hd, hd)]
        return remote(dst, dst, k1_s.at[half, peer], k1_r.at[half, peer], "ctx", peer)

    def kv_own(half):
        src, part = kv_cut(half, c)
        return pltpu.make_async_copy(
            src, kvg.at[c, part, :, pl.ds(half * hd, hd)], own.at[half]
        )

    def q_cut(e, peer):
        return q_hbm.at[:, pl.ds(pl.multiple_of((peer * z.local + e) * hd, hd), hd)]

    def q_one(e, peer):
        return remote(q_cut(e, peer), qg.at[e, c], zq_s.at[e, peer], zq_r.at[e, c], "ctx", peer)

    def q_one_in(e, peer):
        dst = qg.at[e, peer]
        return remote(dst, dst, zq_s.at[e, peer], zq_r.at[e, peer], "ctx", peer)

    def q_own(e):
        return pltpu.make_async_copy(q_cut(e, c), qg.at[e, c], own.at[2 + e])

    def peers(n, me):
        return [lax.rem(me + k, n) for k in alternating(n)]

    for peer in peers(nz, c):
        for half in range(2):
            kv_one(half, peer).start()
    for half in range(2):
        kv_own(half).start()
    for peer in peers(nz, c):
        q_one(0, peer).start()
    q_own(0).start()

    lane = iota((1, 128), 1)
    plan = route_ref[pl.ds(pl.multiple_of(g * z.lanes, z.lanes), z.lanes), :]
    upper = (iota((128, 128), 0) < iota((128, 128), 1)).astype(F32).astype(BF16)
    running = jnp.zeros((nd, 1), F32)
    for i in range(z.lanes):
        mine = (plan[i : i + 1, :] == iota((nd, 128), 0)).astype(F32)
        before = jnp.dot(mine.astype(BF16), upper, preferred_element_type=F32) + running
        rank = jnp.sum(mine * before, axis=0, keepdims=True)
        target[i : i + 1, :] = plan[i : i + 1, :] * z.cap + rank.astype(I32)
        running = running + jnp.sum(mine, axis=1, keepdims=True)

    def pick_batch(j, _):
        first = j * (BATCH * z.cap)
        rows = iota((BATCH * z.cap, 128), 0) + first
        for i in range(z.lanes):
            hit = rows == target[i : i + 1, :]
            pick[j, :, i * 128 : (i + 1) * 128] = jnp.where(hit, 1.0, 0.0).astype(BF16)
        return 0

    lax.fori_loop(0, z.batches, pick_batch, 0)

    arriving = (route_ref[...] == g).astype(F32)
    tally = jnp.sum(arriving.reshape(nd, z.lanes, 128), axis=1)
    count = jnp.sum(tally, axis=1, keepdims=True)
    lower = (iota((nd, nd), 1) < iota((nd, nd), 0)).astype(F32).astype(BF16)
    start = jnp.sum(
        jnp.dot(lower, tally.astype(BF16), preferred_element_type=F32), axis=1, keepdims=True
    )
    live_col[...] = jnp.broadcast_to(jnp.sum(count, axis=0, keepdims=True), (8, 128)).astype(I32)
    count, start = count.astype(I32), start.astype(I32)
    for i in range(z.tiles):
        offset = iota((nd, 128), 1) + i * 128 - z.cap * iota((nd, 128), 0)
        held = (offset >= 0) & (offset < z.cap) & (offset < count)
        slot = jnp.sum(jnp.where(held, (start + offset + 1).astype(F32), 0.0), axis=0, keepdims=True)
        pos[i : i + 1, :] = slot.astype(I32) - 1

    per = z.block // 128

    def tri(b, k):
        return b * z.blocks - (b * (b - 1)) // 2 + (k - b)

    def place_row(b, _):
        rows = iota((z.block, 128), 0) + b * z.block

        def place_one(k, _):
            for i in range(per):
                hit = rows == pos[pl.ds(k * per + i, 1), :]
                place[tri(b, k), :, i * 128 : (i + 1) * 128] = jnp.where(hit, 1.0, 0.0).astype(BF16)
            return 0

        return lax.fori_loop(b, z.blocks, place_one, 0)

    lax.fori_loop(0, z.blocks, place_row, 0)

    lead = z.doc_most // 128
    key_doc[0:lead, :] = jnp.full((lead, 128), -1, I32)
    key_doc[lead : lead + z.tiles, :] = doc_ref[...]
    for i in range(z.tiles):
        row = jnp.broadcast_to(doc_ref[i : i + 1, :].astype(F32), (128, 128))
        query_doc[i * 128 : (i + 1) * 128, :] = row.T.astype(I32)
    pkv[0 : z.doc_most, :] = jnp.zeros((z.doc_most, 2 * hd), BF16)

    for half in range(2):
        kv_own(half).wait()
    for peer in peers(nz, c):
        for half in range(2):
            kv_one_in(half, peer).wait_recv()

    def kv_two(k):
        other = lax.rem(quarter + k, z.team)
        block = kvg.at[:, quarter]
        return remote(block, block, k2_s.at[k], k2_r.at[k], "ctx", quad + other)

    def kv_two_in(k):
        other = lax.rem(quarter - k + z.team, z.team)
        block = kvg.at[:, other]
        return remote(block, block, k2_s.at[k], k2_r.at[k], "ctx", quad + other)

    for k in range(1, z.team):
        kv_two(k).start()
    for e in range(1, z.local):
        for peer in peers(nz, c):
            q_one(e, peer).start()
        q_own(e).start()
    for k in range(1, z.team):
        kv_two_in(k).wait_recv()

    def exchange(rows, send, recv, send_sem, recv_sem, own_sem):
        first = g // BATCH

        def rows_of(ref, s):
            return ref.at[pl.ds(pl.multiple_of(s * z.cap, z.cap), z.cap)]

        def leave(s):
            return remote(rows_of(send, s), rows_of(recv, g), send_sem.at[s], recv_sem.at[g], "dp", s)

        def stay():
            return pltpu.make_async_copy(rows_of(send, g), rows_of(recv, g), own_sem)

        def body(j, _):
            j = lax.rem(first + j, z.batches)
            block = jnp.dot(pick[j], rows, preferred_element_type=F32).astype(BF16)
            height = BATCH * z.cap
            send[pl.ds(pl.multiple_of(j * height, height), height), :] = block
            for i in range(BATCH):
                s = j * BATCH + i

                @pl.when(s != g)
                def _():
                    leave(s).start()

                @pl.when(s == g)
                def _():
                    stay().start()

            return 0

        lax.fori_loop(0, z.batches, body, 0)

        def arrive():
            def body(k, _):
                s = lax.rem(g + k, nd)
                block = rows_of(recv, s)
                remote(block, block, send_sem.at[s], recv_sem.at[s], "dp", s).wait_recv()
                return 0

            stay().wait()
            lax.fori_loop(1, nd, body, 0)

        def finish():
            def body(k, _):
                leave(lax.rem(g + k, nd)).wait_send()
                return 0

            lax.fori_loop(1, nd, body, 0)

        return arrive, finish

    def compact(recv, dst, base, width):
        def body(b, _):
            def inner(k, acc):
                part = recv[pl.ds(pl.multiple_of(k * z.block, z.block), z.block), :]
                return acc + jnp.dot(place[tri(b, k)], part, preferred_element_type=F32)

            acc = lax.fori_loop(b, z.blocks, inner, jnp.zeros((z.block, width), F32))
            dst[pl.ds(pl.multiple_of(base + b * z.block, z.block), z.block), :] = acc.astype(BF16)
            return 0

        lax.fori_loop(0, z.blocks, body, 0)

    factor = float(hd**-0.5 * 1.4426950408889634)
    wide = z.window // 128

    def attend(e):
        def body(b, _):
            at = pl.multiple_of(b * z.block, z.block)
            queries = pq[pl.ds(at, z.block), :]
            keys = pkv[pl.ds(at, z.window), 0:hd]
            scores = lax.dot_general(
                queries, keys, (((1,), (1,)), ((), ())), preferred_element_type=F32
            )
            own_doc = query_doc[pl.ds(at, z.block), :]
            cuts = []
            for i in range(wide):
                ok = own_doc == key_doc[pl.ds(b * per + i, 1), :]
                j = i - (wide - per)
                if j >= 0:
                    ok = ok & (iota((z.block, 128), 1) + j * 128 <= iota((z.block, 128), 0))
                cuts.append(jnp.where(ok, scores[:, i * 128 : (i + 1) * 128], NEG))
            masked = jnp.concatenate(cuts, axis=1)
            top = jnp.max(masked, axis=1, keepdims=True)
            exponent = jnp.exp2((masked - top) * factor)
            total = jnp.sum(exponent, axis=1, keepdims=True)
            values = pkv[pl.ds(at, z.window), hd : 2 * hd]
            mixed = jnp.dot(exponent.astype(BF16), values, preferred_element_type=F32) / total
            alive = iota((z.block, hd), 0) + at < live_col[0:1, :]
            ob[e, pl.ds(at, z.block), :] = jnp.where(alive, mixed, 0.0).astype(BF16)
            return 0

        lax.fori_loop(0, z.blocks, body, 0)

    def out_cols(peer, e):
        return pl.ds(pl.multiple_of((peer * z.local + e) * hd, hd), hd)

    def out_rows(peer, e):
        return ob.at[e, pl.ds(pl.multiple_of(peer * z.slots, z.slots), z.slots)]

    def o_one(e, peer):
        dst = out_ref.at[:, out_cols(c, e)]
        return remote(out_rows(peer, e), dst, o_s.at[e, peer], o_r.at[e, c], "ctx", peer)

    def o_one_in(e, peer):
        dst = out_ref.at[:, out_cols(peer, e)]
        return remote(out_rows(peer, e), dst, o_s.at[e, peer], o_r.at[e, peer], "ctx", peer)

    def o_own(e):
        return pltpu.make_async_copy(
            out_rows(c, e), out_ref.at[:, out_cols(c, e)], own.at[2 + z.local + e]
        )

    kv_rows = kvg[...].reshape(z.group, 2 * hd)
    kv_arrive, kv_finish = exchange(
        kv_rows, send_kv, recv_kv, dkv_s, dkv_r, own.at[2 + 2 * z.local]
    )
    finishes = [kv_finish]
    for e in range(z.local):
        q_own(e).wait()
        for peer in peers(nz, c):
            q_one_in(e, peer).wait_recv()
        q_arrive, q_finish = exchange(
            qg[e].reshape(z.group, hd), send_q.at[e], recv_q.at[e], dq_s.at[e], dq_r.at[e],
            own.at[3 + 2 * z.local + e],
        )
        finishes.append(q_finish)
        if e == 0:
            kv_arrive()
            compact(recv_kv, pkv, z.doc_most, 2 * hd)
        q_arrive()
        compact(recv_q.at[e], pq, 0, hd)
        attend(e)
        for peer in peers(nz, c):
            o_one(e, peer).start()
        o_own(e).start()

    for peer in peers(nz, c):
        for half in range(2):
            kv_one(half, peer).wait_send()
        for e in range(z.local):
            q_one(e, peer).wait_send()
    for k in range(1, z.team):
        kv_two(k).wait_send()
    for finish in finishes:
        finish()
    for e in range(z.local):
        o_own(e).wait()
        for peer in peers(nz, c):
            o_one_in(e, peer).wait_recv()
        for peer in peers(nz, c):
            o_one(e, peer).wait_send()


def call(z, route, docs, q_src, kv_src):
    hd = HEAD_DIM
    dma = pltpu.SemaphoreType.DMA
    vmem = pltpu.VMEM
    tri_blocks = z.blocks * (z.blocks + 1) // 2
    return pl.pallas_call(
        functools.partial(kernel, z),
        out_shape=jax.ShapeDtypeStruct((z.slots, z.heads * hd), BF16),
        in_specs=[
            pl.BlockSpec(memory_space=pltpu.VMEM),
            pl.BlockSpec(memory_space=pltpu.VMEM),
            pl.BlockSpec(memory_space=pl.ANY),
            pl.BlockSpec(memory_space=pl.ANY),
        ],
        out_specs=pl.BlockSpec(memory_space=pl.ANY),
        scratch_shapes=[
            vmem((z.local, z.ctx, z.rows, hd), BF16),
            vmem((z.ctx, z.team, z.part, 2 * hd), BF16),
            vmem((z.local, z.pack, hd), BF16),
            vmem((z.pack, 2 * hd), BF16),
            vmem((z.local, z.pack, hd), BF16),
            vmem((z.pack, 2 * hd), BF16),
            vmem((z.pack, hd), BF16),
            vmem((z.doc_most + z.pack, 2 * hd), BF16),
            vmem((z.local, z.pack, hd), BF16),
            vmem((z.batches, BATCH * z.cap, z.group), BF16),
            vmem((tri_blocks, z.block, z.block), BF16),
            vmem((z.lanes, 128), I32),
            vmem((z.tiles, 128), I32),
            vmem((z.doc_most // 128 + z.tiles, 128), I32),
            vmem((z.pack, 128), I32),
            vmem((8, 128), I32),
            dma((z.local, z.ctx)),
            dma((z.local, z.ctx)),
            dma((2, z.ctx)),
            dma((2, z.ctx)),
            dma((z.team,)),
            dma((z.team,)),
            dma((z.dp,)),
            dma((z.dp,)),
            dma((z.local, z.dp)),
            dma((z.local, z.dp)),
            dma((z.local, z.ctx)),
            dma((z.local, z.ctx)),
            dma((3 + 3 * z.local,)),
        ],
        compiler_params=pltpu.CompilerParams(
            collective_id=0, has_side_effects=True, vmem_limit_bytes=56 << 20
        ),
    )(route, docs, q_src, kv_src)


def on_device(z, q_src, kv_src, route, doc_ids):
    return call(z, route.reshape(-1, 128), doc_ids.reshape(-1, 128), q_src, kv_src)


def solution(mesh):
    z = Sizes(
        mesh.shape["dp"], mesh.shape["ctx"], 128, 96, Q_HEADS, KV_HEADS, DOC_MOST, BLOCK
    )
    in_specs = (P(("dp", "ctx"), None), P(("dp", "ctx"), None), P(), P("dp", None))
    return jax.shard_map(
        functools.partial(on_device, z),
        mesh=mesh,
        in_specs=in_specs,
        out_specs=P(("dp", "ctx"), None),
        check_vma=False,
    )
```

time: 448 us -> 231 us (0.52); the launches traced: 440 us -> 229 us
  Pallas kernels: 0 us -> 227 us
  waiting for transfers between devices: 102 us -> 0 us
  local copies, waits for them, and re-layouts: 92 us -> 2.7 us
  blocking collectives: 75 us -> 0 us
  other arithmetic: 71 us -> 0 us
  matrix products: 49.4 us -> 0 us
  starting transfers between devices: 46.2 us -> 0 us
    pallas_call x0 -> x1, Pallas kernels: none -> 227 us  [call(): pl.pallas_call(functools.partial(kernel, z), out_shape=jax.ShapeDtypeStru...]
    all_to_all x4 -> x0, waiting for transfers between devices: 102 us -> none  [the longest x1 55.4 us: on_device(): lax.all_to_all(wide_pairs, 'ctx', split_axis=1, concat_axis=0, tiled=True)]
    all_to_all x1 -> x0, blocking collectives: 75 us -> none  [on_device(): lax.all_to_all(attended, 'ctx', split_axis=0, concat_axis=1, tiled=True)]
    dot_general x12 -> x0, matrix products: 49.4 us -> none  [the longest x6 33 us: one_block(): jnp.einsum('kgqs,skd->qkgd', weights, key_block[:, 1], preferred_element_...]
    all_to_all x4 -> x0, starting transfers between devices: 46.2 us -> none  [the longest x1 15.7 us: on_device(): lax.all_to_all(q_src, 'ctx', split_axis=1, concat_axis=0, tiled=True)]
    gather x6 -> x0, local copies, waits for them, and re-layouts: 35.5 us -> none  [the longest x2 17.2 us: on_device(): packed_q = jnp.take(recv_q.reshape(pack_len, -1), gather_idx, axis=0)]
    scatter x2 -> x0, local copies, waits for them, and re-layouts: 23 us -> none  [the longest x1 12.1 us: on_device(): jnp.zeros((pack_len, kv_pairs.shape[1]), jnp.bfloat16).at[target]]
    and x7 -> x0, other arithmetic: 22.6 us -> none  [the longest x1 15.7 us: on_device(): packed_q = jnp.take(recv_q.reshape(pack_len, -1), gather_idx, axis=0)]
  transfers between devices with their start and end apart: 4 -> 0, of which waited for: 3 -> 0; matrix products, arithmetic and copies ran while one was open for 23% -> 0% of each run, Pallas kernels for 0% -> 0%
where the time goes in v1:
time: 231 us; the launch traced here: 229 us
  Pallas kernels  227 us (98%)
  local copies, waits for them, and re-layouts  2.7 us (1%)
    pallas_call x1, Pallas kernels, call(): pl.pallas_call(functools.partial(kernel, z), out_shape=jax.ShapeDtypeStru...  227 us

profile of v1, /device:TPU:1, one launch (start us, length us, event | category | flops | bytes accessed | tf_op | source)
XLA Modules:
  0.0 229.3 jit_solution(17215538340252853497)
XLA Ops:
  0.0 226.6 %shard_map.46 = bf16[192,4096]{1,0:T(8,128)(2,1)} custom-call(s32[512,128]{1,0:T(8,128)} %bitcast.2, s32[24,128]{1,0:T(8,128)} %bitcast.3, bf16[128,4096]{1,0:T(8,128)(2,1)} %q_hbm.1, bf16[128,1024]{1,0:T(8,128)(2,1)} %kv_hbm.1), custom_call_target="tpu_custom_call" | custom-call | tf_op jit(solution)/shard_map/pallas_call | solution.py:378
  226.6 2.7 %copy.6 = bf16[192,4096]{1,0:T(8,128)(2,1)} copy(bf16[192,4096]{1,0:T(8,128)(2,1)} %shard_map.46) | data formatting | bytes 3145728

commit v2 on v1

--- a/solution.py
+++ b/solution.py
@@ -1,4 +1,5 @@
 import functools
+import math
 
 import jax
 import jax.numpy as jnp
@@ -36,6 +37,8 @@
         self.blocks = self.pack // block
         self.window = doc_most + block
         self.batches = dp // BATCH
+        self.span = math.gcd(self.pack, 2 * block)
+        self.pieces = math.gcd(self.blocks, 4)
 
 
 def iota(shape, dim):
@@ -150,6 +153,28 @@
 
     lax.fori_loop(0, z.batches, pick_batch, 0)
 
+    for half in range(2):
+        kv_own(half).wait()
+    for peer in peers(nz, c):
+        for half in range(2):
+            kv_one_in(half, peer).wait_recv()
+
+    def kv_two(k):
+        other = lax.rem(quarter + k, z.team)
+        block = kvg.at[:, quarter]
+        return remote(block, block, k2_s.at[k], k2_r.at[k], "ctx", quad + other)
+
+    def kv_two_in(k):
+        other = lax.rem(quarter - k + z.team, z.team)
+        block = kvg.at[:, other]
+        return remote(block, block, k2_s.at[k], k2_r.at[k], "ctx", quad + other)
+
+    for k in range(1, z.team):
+        kv_two(k).start()
+    for e in range(1, z.local):
+        for peer in peers(nz, c):
+            q_one(e, peer).start()
+        q_own(e).start()
     arriving = (route_ref[...] == g).astype(F32)
     tally = jnp.sum(arriving.reshape(nd, z.lanes, 128), axis=1)
     count = jnp.sum(tally, axis=1, keepdims=True)
@@ -167,21 +192,20 @@
 
     per = z.block // 128
 
-    def tri(b, k):
-        return b * z.blocks - (b * (b - 1)) // 2 + (k - b)
-
     def place_row(b, _):
-        rows = iota((z.block, 128), 0) + b * z.block
+        rows = iota((z.span, 128), 0) + b * z.span
 
         def place_one(k, _):
-            for i in range(per):
-                hit = rows == pos[pl.ds(k * per + i, 1), :]
-                place[tri(b, k), :, i * 128 : (i + 1) * 128] = jnp.where(hit, 1.0, 0.0).astype(BF16)
+            hit = rows == pos[pl.ds(k, 1), :]
+            cols = pl.ds(pl.multiple_of(k * 128, 128), 128)
+            place[pl.ds(pl.multiple_of(b * z.span, z.span), z.span), cols] = jnp.where(
+                hit, 1.0, 0.0
+            ).astype(BF16)
             return 0
 
-        return lax.fori_loop(b, z.blocks, place_one, 0)
-
-    lax.fori_loop(0, z.blocks, place_row, 0)
+        return lax.fori_loop(b * (z.span // 128), z.tiles, place_one, 0)
+
+    lax.fori_loop(0, z.pack // z.span, place_row, 0)
 
     lead = z.doc_most // 128
     key_doc[0:lead, :] = jnp.full((lead, 128), -1, I32)
@@ -191,28 +215,6 @@
         query_doc[i * 128 : (i + 1) * 128, :] = row.T.astype(I32)
     pkv[0 : z.doc_most, :] = jnp.zeros((z.doc_most, 2 * hd), BF16)
 
-    for half in range(2):
-        kv_own(half).wait()
-    for peer in peers(nz, c):
-        for half in range(2):
-            kv_one_in(half, peer).wait_recv()
-
-    def kv_two(k):
-        other = lax.rem(quarter + k, z.team)
-        block = kvg.at[:, quarter]
-        return remote(block, block, k2_s.at[k], k2_r.at[k], "ctx", quad + other)
-
-    def kv_two_in(k):
-        other = lax.rem(quarter - k + z.team, z.team)
-        block = kvg.at[:, other]
-        return remote(block, block, k2_s.at[k], k2_r.at[k], "ctx", quad + other)
-
-    for k in range(1, z.team):
-        kv_two(k).start()
-    for e in range(1, z.local):
-        for peer in peers(nz, c):
-            q_one(e, peer).start()
-        q_own(e).start()
     for k in range(1, z.team):
         kv_two_in(k).wait_recv()
 
@@ -267,22 +269,17 @@
 
         return arrive, finish
 
-    def compact(recv, dst, base, width):
-        def body(b, _):
-            def inner(k, acc):
-                part = recv[pl.ds(pl.multiple_of(k * z.block, z.block), z.block), :]
-                return acc + jnp.dot(place[tri(b, k)], part, preferred_element_type=F32)
-
-            acc = lax.fori_loop(b, z.blocks, inner, jnp.zeros((z.block, width), F32))
-            dst[pl.ds(pl.multiple_of(base + b * z.block, z.block), z.block), :] = acc.astype(BF16)
-            return 0
-
-        lax.fori_loop(0, z.blocks, body, 0)
+    def compact(recv, dst, base):
+        for b in range(0, z.pack, z.span):
+            rows = jnp.dot(
+                place[b : b + z.span, b : z.pack], recv[b : z.pack, :], preferred_element_type=F32
+            )
+            dst[base + b : base + b + z.span, :] = rows.astype(BF16)
 
     factor = float(hd**-0.5 * 1.4426950408889634)
     wide = z.window // 128
 
-    def attend(e):
+    def attend(e, first, count):
         def body(b, _):
             at = pl.multiple_of(b * z.block, z.block)
             queries = pq[pl.ds(at, z.block), :]
@@ -308,7 +305,7 @@
             ob[e, pl.ds(at, z.block), :] = jnp.where(alive, mixed, 0.0).astype(BF16)
             return 0
 
-        lax.fori_loop(0, z.blocks, body, 0)
+        lax.fori_loop(first, first + count, body, 0)
 
     def out_cols(peer, e):
         return pl.ds(pl.multiple_of((peer * z.local + e) * hd, hd), hd)
@@ -345,13 +342,25 @@
         finishes.append(q_finish)
         if e == 0:
             kv_arrive()
-            compact(recv_kv, pkv, z.doc_most, 2 * hd)
+            compact(recv_kv, pkv, z.doc_most)
         q_arrive()
-        compact(recv_q.at[e], pq, 0, hd)
-        attend(e)
-        for peer in peers(nz, c):
-            o_one(e, peer).start()
-        o_own(e).start()
+        compact(recv_q.at[e], pq, 0)
+        run, owners = z.blocks // z.pieces, nz // z.pieces
+        home, way = c // owners, 1 + (z.pieces - 2) * lax.rem(c, 2)
+        for turn in range(z.pieces):
+            step = (way, z.pieces // 2, z.pieces - way, 0)[turn] if z.pieces == 4 else turn
+            piece = lax.rem(home + step, z.pieces)
+            attend(e, piece * run, run)
+            for i in range(owners):
+                peer = piece * owners + i
+
+                @pl.when(peer != c)
+                def _():
+                    o_one(e, peer).start()
+
+                @pl.when(peer == c)
+                def _():
+                    o_own(e).start()
 
     for peer in peers(nz, c):
         for half in range(2):
@@ -374,7 +383,6 @@
     hd = HEAD_DIM
     dma = pltpu.SemaphoreType.DMA
     vmem = pltpu.VMEM
-    tri_blocks = z.blocks * (z.blocks + 1) // 2
     return pl.pallas_call(
         functools.partial(kernel, z),
         out_shape=jax.ShapeDtypeStruct((z.slots, z.heads * hd), BF16),
@@ -396,7 +404,7 @@
             vmem((z.doc_most + z.pack, 2 * hd), BF16),
             vmem((z.local, z.pack, hd), BF16),
             vmem((z.batches, BATCH * z.cap, z.group), BF16),
-            vmem((tri_blocks, z.block, z.block), BF16),
+            vmem((z.pack, z.pack), BF16),
             vmem((z.lanes, 128), I32),
             vmem((z.tiles, 128), I32),
             vmem((z.doc_most // 128 + z.tiles, 128), I32),

time: 231 us -> 194 us (0.84)
  Pallas kernels: 227 us -> 191 us
    pallas_call x1, Pallas kernels: 227 us -> 191 us  [call(): pl.pallas_call(functools.partial(kernel, z), out_shape=jax.ShapeDtypeStru...]
where the time goes in v2:
time: 194 us; the launch traced here: 193 us
  Pallas kernels  191 us (98%)
  local copies, waits for them, and re-layouts  2.7 us (1%)
    pallas_call x1, Pallas kernels, call(): pl.pallas_call(functools.partial(kernel, z), out_shape=jax.ShapeDtypeStru...  191 us

profile of v2, /device:TPU:1, one launch (start us, length us, event | category | flops | bytes accessed | tf_op | source)
XLA Modules:
  0.0 193.5 jit_solution(5945945854698914833)
XLA Ops:
  0.0 190.8 %shard_map.46 = bf16[192,4096]{1,0:T(8,128)(2,1)} custom-call(s32[512,128]{1,0:T(8,128)} %bitcast.2, s32[24,128]{1,0:T(8,128)} %bitcast.3, bf16[128,4096]{1,0:T(8,128)(2,1)} %q_hbm.1, bf16[128,1024]{1,0:T(8,128)(2,1)} %kv_hbm.1), custom_call_target="tpu_custom_call" | custom-call | tf_op jit(solution)/shard_map/pallas_call | solution.py:386
  190.8 2.7 %copy.6 = bf16[192,4096]{1,0:T(8,128)(2,1)} copy(bf16[192,4096]{1,0:T(8,128)(2,1)} %shard_map.46) | data formatting | bytes 3145728

commit v3 on v2

--- a/solution.py
+++ b/solution.py
@@ -47,16 +47,16 @@
 
 def alternating(n):
     order = []
-    for k in range(1, n // 2):
+    for k in range(n // 2 - 1, 0, -1):
         order += [k, n - k]
-    return order + [n // 2]
+    return order
 
 
 def kernel(
     z, route_ref, doc_ref, q_hbm, kv_hbm, out_ref,
     qg, kvg, send_q, send_kv, recv_q, recv_kv, pq, pkv, ob, pick, place,
-    target, pos, key_doc, query_doc, live_col,
-    zq_s, zq_r, k1_s, k1_r, k2_s, k2_r, dkv_s, dkv_r, dq_s, dq_r, o_s, o_r, own,
+    target, pos, key_doc, query_doc, live_col, relay_q, relay_o,
+    hop_s, hop_r, end_s, end_r, zq_s, zq_r, k1_s, k1_r, k2_s, k2_r, dkv_s, dkv_r, dq_s, dq_r, o_s, o_r, own,
 ):
     g = lax.axis_index("dp")
     c = lax.axis_index("ctx")
@@ -123,14 +123,52 @@
     def peers(n, me):
         return [lax.rem(me + k, n) for k in alternating(n)]
 
-    for peer in peers(nz, c):
+    facing = lax.rem(c + nz // 2, nz)
+    turns = (nz // 4, nz - nz // 4)
+
+    def half_of(ref, way, n):
+        return ref.at[pl.ds(way * (n // 2), n // 2)]
+
+    def hop(block, relay, kind, e, way):
+        peer = lax.rem(c + turns[way], nz)
+        return remote(
+            block, relay.at[e, way], hop_s.at[kind, e, way], hop_r.at[kind, e, way], "ctx", peer
+        )
+
+    def hand_on(relay, dst, kind, e, way):
+        peer = lax.rem(c + turns[way], nz)
+        return remote(
+            relay.at[e, way], dst, end_s.at[kind, e, way], end_r.at[kind, e, way], "ctx", peer
+        )
+
+    def q_hop(e, way):
+        return hop(half_of(q_cut(e, facing), way, z.rows), relay_q, 0, e, way)
+
+    def q_pass(e, way):
+        origin = lax.rem(c + turns[1 - way], nz)
+        return hand_on(relay_q, half_of(qg.at[e, origin], way, z.rows), 0, e, way)
+
+    def q_end(e, way):
+        return hand_on(relay_q, half_of(qg.at[e, facing], way, z.rows), 0, e, way)
+
+    def send_q_rows(e):
+        for way in range(2):
+            q_hop(e, way).start()
+        for peer in peers(nz, c):
+            q_one(e, peer).start()
+        q_own(e).start()
+
+    def pass_q_rows(e):
+        for way in range(2):
+            q_hop(e, way).wait_recv()
+            q_pass(e, way).start()
+
+    for peer in peers(nz, c) + [facing]:
         for half in range(2):
             kv_one(half, peer).start()
     for half in range(2):
         kv_own(half).start()
-    for peer in peers(nz, c):
-        q_one(0, peer).start()
-    q_own(0).start()
+    send_q_rows(0)
 
     lane = iota((1, 128), 1)
     plan = route_ref[pl.ds(pl.multiple_of(g * z.lanes, z.lanes), z.lanes), :]
@@ -155,7 +193,7 @@
 
     for half in range(2):
         kv_own(half).wait()
-    for peer in peers(nz, c):
+    for peer in peers(nz, c) + [facing]:
         for half in range(2):
             kv_one_in(half, peer).wait_recv()
 
@@ -171,10 +209,9 @@
 
     for k in range(1, z.team):
         kv_two(k).start()
+    pass_q_rows(0)
     for e in range(1, z.local):
-        for peer in peers(nz, c):
-            q_one(e, peer).start()
-        q_own(e).start()
+        send_q_rows(e)
     arriving = (route_ref[...] == g).astype(F32)
     tally = jnp.sum(arriving.reshape(nd, z.lanes, 128), axis=1)
     count = jnp.sum(tally, axis=1, keepdims=True)
@@ -326,6 +363,23 @@
             out_rows(c, e), out_ref.at[:, out_cols(c, e)], own.at[2 + z.local + e]
         )
 
+    def o_hop(e, way):
+        return hop(half_of(out_rows(facing, e), way, z.slots), relay_o, 1, e, way)
+
+    def o_pass(e, way):
+        origin = lax.rem(c + turns[1 - way], nz)
+        dst = half_of(out_ref, way, z.slots).at[:, out_cols(origin, e)]
+        return hand_on(relay_o, dst, 1, e, way)
+
+    def o_end(e, way):
+        dst = half_of(out_ref, way, z.slots).at[:, out_cols(facing, e)]
+        return hand_on(relay_o, dst, 1, e, way)
+
+    def pass_outputs(e):
+        for way in range(2):
+            o_hop(e, way).wait_recv()
+            o_pass(e, way).start()
+
     kv_rows = kvg[...].reshape(z.group, 2 * hd)
     kv_arrive, kv_finish = exchange(
         kv_rows, send_kv, recv_kv, dkv_s, dkv_r, own.at[2 + 2 * z.local]
@@ -335,11 +389,17 @@
         q_own(e).wait()
         for peer in peers(nz, c):
             q_one_in(e, peer).wait_recv()
+        for way in range(2):
+            q_end(e, way).wait_recv()
         q_arrive, q_finish = exchange(
             qg[e].reshape(z.group, hd), send_q.at[e], recv_q.at[e], dq_s.at[e], dq_r.at[e],
             own.at[3 + 2 * z.local + e],
         )
         finishes.append(q_finish)
+        if e > 0:
+            pass_outputs(e - 1)
+        if e + 1 < z.local:
+            pass_q_rows(e + 1)
         if e == 0:
             kv_arrive()
             compact(recv_kv, pkv, z.doc_most)
@@ -348,31 +408,45 @@
         run, owners = z.blocks // z.pieces, nz // z.pieces
         home, way = c // owners, 1 + (z.pieces - 2) * lax.rem(c, 2)
         for turn in range(z.pieces):
-            step = (way, z.pieces // 2, z.pieces - way, 0)[turn] if z.pieces == 4 else turn
+            step = (z.pieces // 2, way, z.pieces - way, 0)[turn] if z.pieces == 4 else turn
             piece = lax.rem(home + step, z.pieces)
             attend(e, piece * run, run)
             for i in range(owners):
                 peer = piece * owners + i
 
-                @pl.when(peer != c)
+                @pl.when((peer != c) & (peer != facing))
                 def _():
                     o_one(e, peer).start()
+
+                @pl.when(peer == facing)
+                def _():
+                    for way in range(2):
+                        o_hop(e, way).start()
 
                 @pl.when(peer == c)
                 def _():
                     o_own(e).start()
 
-    for peer in peers(nz, c):
+    pass_outputs(z.local - 1)
+    for peer in peers(nz, c) + [facing]:
         for half in range(2):
             kv_one(half, peer).wait_send()
-        for e in range(z.local):
+    for e in range(z.local):
+        for peer in peers(nz, c):
             q_one(e, peer).wait_send()
+        for way in range(2):
+            q_hop(e, way).wait_send()
+            q_pass(e, way).wait_send()
+            o_hop(e, way).wait_send()
+            o_pass(e, way).wait_send()
     for k in range(1, z.team):
         kv_two(k).wait_send()
     for finish in finishes:
         finish()
     for e in range(z.local):
         o_own(e).wait()
+        for way in range(2):
+            o_end(e, way).wait_recv()
         for peer in peers(nz, c):
             o_one_in(e, peer).wait_recv()
         for peer in peers(nz, c):
@@ -410,6 +484,12 @@
             vmem((z.doc_most // 128 + z.tiles, 128), I32),
             vmem((z.pack, 128), I32),
             vmem((8, 128), I32),
+            vmem((z.local, 2, z.rows // 2, hd), BF16),
+            vmem((z.local, 2, z.slots // 2, hd), BF16),
+            dma((2, z.local, 2)),
+            dma((2, z.local, 2)),
+            dma((2, z.local, 2)),
+            dma((2, z.local, 2)),
             dma((z.local, z.ctx)),
             dma((z.local, z.ctx)),
             dma((2, z.ctx)),

time: 194 us -> 194 us (level)
  Pallas kernels: 191 us -> 189 us
where the time goes in v3:
time: 194 us; the launch traced here: 192 us
  Pallas kernels  189 us (97%)
  local copies, waits for them, and re-layouts  2.7 us (1%)
    pallas_call x1, Pallas kernels, call(): pl.pallas_call(functools.partial(kernel, z), out_shape=jax.ShapeDtypeStru...  189 us

profile of v3, /device:TPU:1, one launch (start us, length us, event | category | flops | bytes accessed | tf_op | source)
XLA Modules:
  0.0 191.7 jit_solution(16005886281420932152)
XLA Ops:
  0.0 189.0 %shard_map.46 = bf16[192,4096]{1,0:T(8,128)(2,1)} custom-call(s32[512,128]{1,0:T(8,128)} %bitcast.2, s32[24,128]{1,0:T(8,128)} %bitcast.3, bf16[128,4096]{1,0:T(8,128)(2,1)} %q_hbm.1, bf16[128,1024]{1,0:T(8,128)(2,1)} %kv_hbm.1), custom_call_target="tpu_custom_call" | custom-call | tf_op jit(solution)/shard_map/pallas_call | solution.py:460
  189.0 2.7 %copy.6 = bf16[192,4096]{1,0:T(8,128)(2,1)} copy(bf16[192,4096]{1,0:T(8,128)(2,1)} %shard_map.46) | data formatting | bytes 3145728

commit v4 on v3

--- a/solution.py
+++ b/solution.py
@@ -168,7 +168,6 @@
             kv_one(half, peer).start()
     for half in range(2):
         kv_own(half).start()
-    send_q_rows(0)
 
     lane = iota((1, 128), 1)
     plan = route_ref[pl.ds(pl.multiple_of(g * z.lanes, z.lanes), z.lanes), :]
@@ -209,9 +208,6 @@
 
     for k in range(1, z.team):
         kv_two(k).start()
-    pass_q_rows(0)
-    for e in range(1, z.local):
-        send_q_rows(e)
     arriving = (route_ref[...] == g).astype(F32)
     tally = jnp.sum(arriving.reshape(nd, z.lanes, 128), axis=1)
     count = jnp.sum(tally, axis=1, keepdims=True)
@@ -254,6 +250,7 @@
 
     for k in range(1, z.team):
         kv_two_in(k).wait_recv()
+    send_q_rows(0)
 
     def exchange(rows, send, recv, send_sem, recv_sem, own_sem):
         first = g // BATCH
@@ -385,12 +382,15 @@
         kv_rows, send_kv, recv_kv, dkv_s, dkv_r, own.at[2 + 2 * z.local]
     )
     finishes = [kv_finish]
+    pass_q_rows(0)
     for e in range(z.local):
         q_own(e).wait()
         for peer in peers(nz, c):
             q_one_in(e, peer).wait_recv()
         for way in range(2):
             q_end(e, way).wait_recv()
+        if e + 1 < z.local:
+            send_q_rows(e + 1)
         q_arrive, q_finish = exchange(
             qg[e].reshape(z.group, hd), send_q.at[e], recv_q.at[e], dq_s.at[e], dq_r.at[e],
             own.at[3 + 2 * z.local + e],
@@ -398,12 +398,12 @@
         finishes.append(q_finish)
         if e > 0:
             pass_outputs(e - 1)
-        if e + 1 < z.local:
-            pass_q_rows(e + 1)
         if e == 0:
             kv_arrive()
             compact(recv_kv, pkv, z.doc_most)
         q_arrive()
+        if e + 1 < z.local:
+            pass_q_rows(e + 1)
         compact(recv_q.at[e], pq, 0)
         run, owners = z.blocks // z.pieces, nz // z.pieces
         home, way = c // owners, 1 + (z.pieces - 2) * lax.rem(c, 2)

time: 194 us -> 188 us (0.969)
  Pallas kernels: 189 us -> 185 us
    pallas_call x1, Pallas kernels: 189 us -> 185 us  [call(): pl.pallas_call(functools.partial(kernel, z), out_shape=jax.ShapeDtypeStru...]
where the time goes in v4:
time: 188 us; the launch traced here: 187 us
  Pallas kernels  185 us (98%)
  local copies, waits for them, and re-layouts  2.7 us (1%)
    pallas_call x1, Pallas kernels, call(): pl.pallas_call(functools.partial(kernel, z), out_shape=jax.ShapeDtypeStru...  185 us

profile of v4, /device:TPU:1, one launch (start us, length us, event | category | flops | bytes accessed | tf_op | source)
XLA Modules:
  0.0 187.4 jit_solution(7786768100355946161)
XLA Ops:
  0.0 184.6 %shard_map.46 = bf16[192,4096]{1,0:T(8,128)(2,1)} custom-call(s32[512,128]{1,0:T(8,128)} %bitcast.2, s32[24,128]{1,0:T(8,128)} %bitcast.3, bf16[128,4096]{1,0:T(8,128)(2,1)} %q_hbm.1, bf16[128,1024]{1,0:T(8,128)(2,1)} %kv_hbm.1), custom_call_target="tpu_custom_call" | custom-call | tf_op jit(solution)/shard_map/pallas_call | solution.py:460
  184.7 2.7 %copy.6 = bf16[192,4096]{1,0:T(8,128)(2,1)} copy(bf16[192,4096]{1,0:T(8,128)(2,1)} %shard_map.46) | data formatting | bytes 3145728

commit v5 on v4

--- a/solution.py
+++ b/solution.py
@@ -208,6 +208,7 @@
 
     for k in range(1, z.team):
         kv_two(k).start()
+    send_q_rows(0)
     arriving = (route_ref[...] == g).astype(F32)
     tally = jnp.sum(arriving.reshape(nd, z.lanes, 128), axis=1)
     count = jnp.sum(tally, axis=1, keepdims=True)
@@ -250,7 +251,7 @@
 
     for k in range(1, z.team):
         kv_two_in(k).wait_recv()
-    send_q_rows(0)
+    pass_q_rows(0)
 
     def exchange(rows, send, recv, send_sem, recv_sem, own_sem):
         first = g // BATCH
@@ -382,7 +383,6 @@
         kv_rows, send_kv, recv_kv, dkv_s, dkv_r, own.at[2 + 2 * z.local]
     )
     finishes = [kv_finish]
-    pass_q_rows(0)
     for e in range(z.local):
         q_own(e).wait()
         for peer in peers(nz, c):

time: 188 us -> 183 us (0.973); the launches traced: 187 us -> 180 us
  Pallas kernels: 185 us -> 178 us
    pallas_call x1, Pallas kernels: 185 us -> 178 us  [call(): pl.pallas_call(functools.partial(kernel, z), out_shape=jax.ShapeDtypeStru...]
where the time goes in v5:
time: 183 us; the launch traced here: 180 us
  Pallas kernels  178 us (97%)
  local copies, waits for them, and re-layouts  2.7 us (1%)
    pallas_call x1, Pallas kernels, call(): pl.pallas_call(functools.partial(kernel, z), out_shape=jax.ShapeDtypeStru...  178 us

profile of v5, /device:TPU:1, one launch (start us, length us, event | category | flops | bytes accessed | tf_op | source)
XLA Modules:
  0.0 180.4 jit_solution(7044944774997317863)
XLA Ops:
  0.0 177.7 %shard_map.46 = bf16[192,4096]{1,0:T(8,128)(2,1)} custom-call(s32[512,128]{1,0:T(8,128)} %bitcast.2, s32[24,128]{1,0:T(8,128)} %bitcast.3, bf16[128,4096]{1,0:T(8,128)(2,1)} %q_hbm.1, bf16[128,1024]{1,0:T(8,128)(2,1)} %kv_hbm.1), custom_call_target="tpu_custom_call" | custom-call | tf_op jit(solution)/shard_map/pallas_call | solution.py:460
  177.7 2.7 %copy.6 = bf16[192,4096]{1,0:T(8,128)(2,1)} copy(bf16[192,4096]{1,0:T(8,128)(2,1)} %shard_map.46) | data formatting | bytes 3145728
